TPU v7x, 256 devices: a whole 4x4x8 slice. The times are simulated.
256 devices in a mesh: row: 8 (over y, core), col: 32 (over x, z).
Axes of the slice: x: 4, y: 4, z: 8, core: 2. Of those that a mesh axis runs over, the one named last changes fastest.
Arguments:
- sources: float32 [65536, 256], P(('row', 'col')), may hold values from -6 to 6
- targets: float32 [65536, 256], P(('col', 'row')), may hold values from -6 to 6
- g_pot: float32 [65536], P(('col', 'row')), may hold values from -1 to 12
- log_a: float32 [65536], P(('row', 'col')), may hold values from -14 to -8
- log_b: float32 [65536], P(('col', 'row')), may hold values from -14 to -8
- src_block: int32 [16384], P(('row', 'col')), may hold values from 0 to 31, as said below
- tgt_block: int32 [16384], P(('row', 'col')), may hold values from 0 to 7, as said below
- pair_count: int32 [256], P(('row', 'col')), may hold values from 16 to 64, as said below
Outputs:
- f_new: float32 [65536], P(('row', 'col'))
- g_new: float32 [65536], P(('col', 'row'))
Inputs may be any that keep to these rules, and one draw needn't show every extreme that they name: `src_block`: within each row index, slot 0 of the 32 devices names together every source block of that row index once; slot k and slot k + 32 of a device name the same source block. `tgt_block`: within each col index, slot 0 of the 8 devices names together every target block of that col index once. `pair_count`: some device has all 64 slots live.
All inputs are finite; a program needn't handle non-finite values.
Results may differ from a plain program's by a relative error of at most 0.0003.
Values sent between devices are 32-bit elements; how exact they have to be, the bound alone decides.
A program may use at most 128 MiB of HBM per device.

v0:
```python
import jax
import jax.numpy as jnp
from jax import lax
from jax.sharding import PartitionSpec as P

BLK = 256
entropy = 0.05
lowest = -1e30


def squares_of(rows):
    return jnp.sum(rows * rows, axis=-1)


def cost_blocks(src_rows, tgt_rows, src_sq, tgt_sq):
    inner = jnp.einsum("kid,kjd->kij", src_rows, tgt_rows, precision=lax.Precision.HIGHEST)
    return (src_sq[:, :, None] + tgt_sq[:, None, :] - 2.0 * inner) / src_rows.shape[2]


def fold_blocks(slot_top, slot_total, slot_ids, alive, count):
    onehot = (slot_ids[:, None] == jnp.arange(count, dtype=jnp.int32)[None, :]) & alive[:, None]
    masked = jnp.where(onehot.T[:, :, None], slot_top[None, :, :], lowest)
    top = jnp.max(masked, axis=1)
    back = jnp.take(top, slot_ids, axis=0)
    weighted = jnp.where(alive[:, None], slot_total * jnp.exp(slot_top - back), 0.0)
    total = jnp.dot(onehot.T.astype(jnp.float32), weighted, precision=lax.Precision.HIGHEST)
    return (top.reshape(-1), total.reshape(-1))


def local(sources, targets, g_pot, log_a, log_b, src_block, tgt_block, pair_count):
    used_pairs = pair_count[0]
    slots = src_block.shape[0]
    alive = jnp.arange(slots, dtype=jnp.int32) < used_pairs
    tgt_all, pot_all = (
        lax.all_gather(targets, "row", axis=0, tiled=True),
        lax.all_gather(g_pot, "row", axis=0, tiled=True),
    )
    src_all, weight_all = (
        lax.all_gather(sources, "col", axis=0, tiled=True),
        lax.all_gather(log_a, "col", axis=0, tiled=True),
    )
    width = sources.shape[1]
    src_count = src_all.shape[0] // BLK
    tgt_count = tgt_all.shape[0] // BLK
    src_blocks = src_all.reshape(src_count, BLK, width)
    tgt_blocks = tgt_all.reshape(tgt_count, BLK, width)
    src_sq_all = squares_of(src_blocks)
    tgt_sq_all = squares_of(tgt_blocks)
    src_rows = jnp.take(src_blocks, src_block, axis=0)
    tgt_rows = jnp.take(tgt_blocks, tgt_block, axis=0)
    src_sq = jnp.take(src_sq_all, src_block, axis=0)
    tgt_sq = jnp.take(tgt_sq_all, tgt_block, axis=0)
    pot_rows = jnp.take(pot_all.reshape(tgt_count, BLK), tgt_block, axis=0)
    costs = cost_blocks(src_rows, tgt_rows, src_sq, tgt_sq)
    scores = (pot_rows[:, None, :] - costs) / entropy
    slot_top = jnp.max(scores, axis=2)
    slot_total = jnp.sum(jnp.exp(scores - slot_top[:, :, None]), axis=2)
    src_top, src_total = fold_blocks(slot_top, slot_total, src_block, alive, src_count)
    whole_top = lax.pmax(src_top, "col")
    src_total = lax.psum(src_total * jnp.exp(src_top - whole_top), "col")
    src_top = whole_top
    f_all = entropy * weight_all - entropy * (src_top + jnp.log(src_total))
    second_costs = cost_blocks(src_rows, tgt_rows, src_sq, tgt_sq)
    f_rows = jnp.take(f_all.reshape(src_count, BLK), src_block, axis=0)
    back_scores = (f_rows[:, :, None] - second_costs) / entropy
    col_top = jnp.max(back_scores, axis=1)
    col_total = jnp.sum(jnp.exp(back_scores - col_top[:, None, :]), axis=1)
    tgt_top, tgt_total = fold_blocks(col_top, col_total, tgt_block, alive, tgt_count)
    whole_tgt = lax.pmax(tgt_top, "row")
    tgt_total = lax.psum(tgt_total * jnp.exp(tgt_top - whole_tgt), "row")
    tgt_top = whole_tgt
    own_src = sources.shape[0]
    own_tgt = targets.shape[0]
    f_own = lax.dynamic_slice_in_dim(f_all, lax.axis_index("col") * own_src, own_src, 0)
    tgt_offset = lax.axis_index("row") * own_tgt
    top_own = lax.dynamic_slice_in_dim(tgt_top, tgt_offset, own_tgt, 0)
    total_own = lax.dynamic_slice_in_dim(tgt_total, tgt_offset, own_tgt, 0)
    g_own = entropy * log_b - entropy * (top_own + jnp.log(total_own))
    return (f_own, g_own)


def solution(mesh):
    placed = (
        P(("row", "col"), None),
        P(("col", "row"), None),
        P(("col", "row")),
        P(("row", "col")),
        P(("col", "row")),
        P(("row", "col")),
        P(("row", "col")),
        P(("row", "col")),
    )
    return jax.shard_map(
        local,
        mesh=mesh,
        in_specs=placed,
        out_specs=(P(("row", "col")), P(("col", "row"))),
        check_vma=False,
    )
```

profile of v0, /device:TPU:1, one launch (start us, length us, event | category | flops | bytes accessed | tf_op | source)
XLA Modules:
  0.0 527.1 jit_solution(1191801241612126786)
XLA Ops:
  7.2 0.0 all-gather.7.cloned.1.call-start
  7.2 0.7 all-gather.7.cloned.1.call-update
  7.9 0.0 all-gather.5.cloned.1.call-start
  7.9 0.7 all-gather.5.cloned.1.call-update
  8.7 12.4 %all-gather.1 = f32[8,1,256]{2,1,0:T(1,128)S(1)} all-gather(f32[1,1,256]{2,1,0:T(1,128)} %bitcast.32), channel_id=1, replica_groups=mesh['row'=8,'col'=32] {'row'}, dimensions={0}, use_global_device_ids=true | all-gather | bytes 9216 | tf_op jit(solution)/shard_map/all_gather | solution.py:36
  21.7 0.7 compare_select_fusion.1
  22.4 0.7 gather_fusion.2
  23.0 37.7 %all-gather = f32[32,1,256]{2,1,0:T(1,128)S(1)} all-gather(f32[1,1,256]{2,1,0:T(1,128)} %bitcast.33), channel_id=1, replica_groups=mesh['row'=8,'col'=32] {'col'}, dimensions={0}, use_global_device_ids=true | all-gather | bytes 33792 | tf_op jit(solution)/shard_map/all_gather | solution.py:40
  60.8 0.7 compare_select_fusion
  61.4 0.7 compare_and_fusion.1
  62.1 0.7 compare_and_fusion
  62.8 0.7 fusion.37
  63.4 0.7 fusion.36
  64.1 0.0 all-gather.7.cloned.1.call-done
  64.2 1.9 multiply_reduce_fusion.1
  66.1 0.7 gather_fusion.4
  66.8 10.5 %gather_fusion.1 = f32[64,256,256]{2,1,0:T(8,128)} fusion(f32[8,256,256]{2,1,0:T(8,128)} %bitcast.20, s32[1024]{0:T(1024)S(1)} %pad_clamp_fusion.1), kind=kCustom, calls=%fused_computation.7 | custom fusion | bytes 33554688 | tf_op jit(solution)/shard_map/jit(_take)/gather | solution.py:50
  77.3 0.1 broadcast_select_fusion.3
  77.3 64.3 %all-gather.5.cloned.1.call-done = f32[8192,256]{1,0:T(8,128)} async-done(((f32[256,256]{1,0:T(8,128)}), f32[8192,256]{1,0:T(8,128)}) %all-gather.5.cloned.1.call-update) | async-done | bytes 8388624 | tf_op jit(solution)/shard_map/all_gather | solution.py:39
  141.6 4.5 multiply_reduce_fusion
  146.2 0.7 gather_fusion.3
  146.8 11.6 %gather_fusion = f32[64,256,256]{2,1,0:T(8,128)} fusion(f32[32,256,256]{2,1,0:T(8,128)} %bitcast.21, s32[1024]{0:T(1024)S(1)} %pad_clamp_fusion), kind=kCustom, calls=%fused_computation.6 | custom fusion | bytes 33554688 | tf_op jit(solution)/shard_map/jit(_take)/gather | solution.py:49
  158.5 0.1 broadcast_select_fusion.2
  158.5 29.9 %fusion.3 = (f32[64,256]{1,0:T(8,128)S(1)}, f32[64,256,256]{2,1,0:T(8,128)}) fusion(f32[64,256]{1,0:T(8,128)S(1)} %get-tuple-element.4, f32[64,256,256]{2,1,0:T(8,128)} %gather_fusion.1, pred[64]{0:T(512)(128)(4,1)S(1)} %compare_and_fusion.1, f32[64,256,256]{2,1,0:T(8,128)} %gather_fusion, pred[64]{0:T(512)(128)(4,1)S(1)} %compare_and_fusion, ...), kind=kOutput, calls=%fused_computation.16 | convolution fusion | flops 12922634240 | bytes 50593920 | tf_op jit(solution)/shard_map/kid,kjd->kij/dot_general | solution.py:16
  188.4 0.0 copy-start.1
  188.4 8.5 %exponential_reduce_fusion.1 = f32[64,256]{1,0:T(8,128)S(1)} fusion(f32[64,256,256]{2,1,0:T(8,128)} %get-tuple-element.7, f32[64,256]{1,0:T(8,128)S(1)} %get-tuple-element.6, f32[64,256]{1,0:T(8,128)S(1)} %get-tuple-element.4), kind=kLoop, calls=%fused_computation.10 | loop fusion | flops 16760832 | bytes 16973824 | tf_op jit(solution)/shard_map/reduce_sum | solution.py:57
  197.0 0.5 select_reduce_fusion
  197.5 0.7 gather_fusion.5
  198.2 0.0 copy-done.1
  198.2 0.3 convolution_bitcast_fusion
  198.5 111.5 %pmax.14 = f32[8192]{0:T(1024)S(1)} all-reduce(f32[8192]{0:T(1024)S(1)} %bitcast.25), channel_id=1, replica_groups=mesh['row'=8,'col'=32] {'col'}, use_global_device_ids=true, to_apply=%region_4.7 | all-reduce | flops 8192 | bytes 65536 | tf_op jit(solution)/shard_map/pmax | solution.py:59
  310.0 110.7 %psum.14 = f32[8192]{0:T(1024)S(1)} all-reduce(f32[8192]{0:T(1024)S(1)} %exponential_multiply_fusion), channel_id=1, replica_groups=mesh['row'=8,'col'=32] {'col'}, use_global_device_ids=true, to_apply=%region_6.9 | all-reduce | flops 8192 | bytes 65536 | tf_op jit(solution)/shard_map/psum | solution.py:60
  420.8 0.7 gather_fusion.6
  421.4 0.1 broadcast_select_fusion
  421.5 0.0 copy-start.2
  421.5 0.0 copy-start
  421.5 7.2 %fusion.4 = f32[64,256]{1,0:T(8,128)S(1)} fusion(f32[64,256,256]{2,1,0:T(8,128)} %get-tuple-element.7, f32[64,256]{1,0:T(8,128)S(1)} %broadcast_select_fusion), kind=kLoop, calls=%fused_computation.17 | loop fusion | flops 12566528 | bytes 16908288 | tf_op jit(solution)/shard_map/reduce_max | solution.py:66
  428.8 8.0 %exponential_reduce_fusion = f32[64,256]{1,0:T(8,128)S(1)} fusion(f32[64,256,256]{2,1,0:T(8,128)} %get-tuple-element.7, f32[64,256]{1,0:T(8,128)S(1)} %fusion.4, f32[64,256]{1,0:T(8,128)S(1)} %broadcast_select_fusion), kind=kLoop, calls=%fused_computation.8 | loop fusion | flops 16760832 | bytes 16973824 | tf_op jit(solution)/shard_map/reduce_sum | solution.py:67
  436.8 0.1 select_reduce_fusion.1
  437.0 0.7 gather_fusion.7
  437.6 0.0 copy-done.2
  437.6 0.3 convolution_bitcast_fusion.1
  437.9 68.4 %pmax.15 = f32[2048]{0:T(1024)S(1)} all-reduce(f32[2048]{0:T(1024)S(1)} %bitcast.29), channel_id=1, replica_groups=mesh['row'=8,'col'=32] {'row'}, use_global_device_ids=true, to_apply=%region_9.12 | all-reduce | flops 2048 | bytes 16384 | tf_op jit(solution)/shard_map/pmax | solution.py:69
  506.3 12.7 %psum.15 = f32[2048]{0:T(1024)S(1)} all-reduce(f32[2048]{0:T(1024)S(1)} %exponential_multiply_fusion.1), channel_id=1, replica_groups=mesh['row'=8,'col'=32] {'row'}, use_global_device_ids=true, to_apply=%region_11.14 | all-reduce | flops 2048 | bytes 16384 | tf_op jit(solution)/shard_map/psum | solution.py:70
  519.0 0.6 dynamic_slice.9
  519.7 0.0 copy-done
  519.7 0.6 multiply_subtract_fusion.1
  (15 shorter events, 0.2 us)
Async XLA Ops:
  7.2 57.0 %all-gather.7.cloned.1.call-start = ((), (), s32[]{:S(2)}) async-start(), calls=%async_computation.1 | async-start | bytes 2359296 | tf_op jit(solution)/shard_map/all_gather | solution.py:35
  7.9 133.7 %all-gather.5.cloned.1.call-start = ((), (), s32[]{:S(2)}) async-start(), calls=%async_computation | async-start | bytes 8650752 | tf_op jit(solution)/shard_map/all_gather | solution.py:39
  188.4 9.7 %copy-start.1 = (s32[64]{0:T(128)S(1)}, s32[64]{0:T(128)}, u32[]{:S(2)}) copy-start(s32[64]{0:T(128)} %param.17) | copy-start | bytes 772
  421.5 16.1 %copy-start.2 = (s32[64]{0:T(128)S(1)}, s32[64]{0:T(128)}, u32[]{:S(2)}) copy-start(s32[64]{0:T(128)} %param.18) | copy-start | bytes 772
  421.5 98.1 %copy-start = (f32[256]{0:T(256)S(1)}, f32[256]{0:T(256)}, u32[]{:S(2)}) copy-start(f32[256]{0:T(256)} %param.16) | copy-start | bytes 3076
Sparse Core Ops, SparseCore 0:
  9.8 32.0 all-gather.6
  44.5 97.0 all-gather.4
where the time goes:
time: 528 us; the launch traced here: 527 us
  blocking collectives  353 us (67%)
  waiting for transfers between devices  65.7 us (12%)
  other arithmetic  35.9 us (7%)
  matrix products  30.4 us (6%)
  local copies, waits for them, and re-layouts  26.8 us (5%)
  between operations  14.9 us (3%)
    pmax x1, blocking collectives, local(): whole_top = lax.pmax(src_top, 'col')  112 us
    psum x1, blocking collectives, local(): src_total = lax.psum(src_total * jnp.exp(src_top - whole_top), 'col')  111 us
    pmax x1, blocking collectives, local(): whole_tgt = lax.pmax(tgt_top, 'row')  68.4 us
    all_gather x1, waiting for transfers between devices, local(): lax.all_gather(sources, 'col', axis=0, tiled=True)  64.3 us
    all_gather x1, blocking collectives, local(): lax.all_gather(log_a, 'col', axis=0, tiled=True)  37.7 us
    dot_general x1, matrix products, cost_blocks(): jnp.einsum('kid,kjd->kij', src_rows, tgt_rows, precision=lax.Precision.HI...  29.9 us
    psum x1, blocking collectives, local(): tgt_total = lax.psum(tgt_total * jnp.exp(tgt_top - whole_tgt), 'row')  12.7 us
    all_gather x1, blocking collectives, local(): lax.all_gather(g_pot, 'row', axis=0, tiled=True)  12.4 us
  transfers between devices with their start and end apart: 2, of which 1 were waited for; matrix products, arithmetic and copies ran while one was open for 3% of the time, Pallas kernels for 0%

commit v1 on v0

--- a/solution.py
+++ b/solution.py
@@ -37,7 +37,9 @@
     )
     src_all, weight_all = (
         lax.all_gather(sources, "col", axis=0, tiled=True),
-        lax.all_gather(log_a, "col", axis=0, tiled=True),
+        jnp.concatenate(
+            lax.all_to_all(jnp.stack([log_a] * lax.axis_size("col")), "col", 0, 0), axis=0
+        ),
     )
     width = sources.shape[1]
     src_count = src_all.shape[0] // BLK

time: 528 us -> 528 us (level)
  blocking collectives: 353 us -> 315 us
  waiting for transfers between devices: 65.7 us -> 90.7 us
  starting transfers between devices: 0.08 us -> 11.9 us
    all_gather x1 -> x0, blocking collectives: 37.7 us -> none  [local(): lax.all_gather(log_a, 'col', axis=0, tiled=True)]
    all_gather x1, waiting for transfers between devices: 64.3 us -> 86.5 us  [local(): lax.all_gather(sources, 'col', axis=0, tiled=True)]
    all_to_all x0 -> x1, starting transfers between devices: none -> 11.9 us  [local(): lax.all_to_all(jnp.stack([log_a] * lax.axis_size('col')), 'col', 0, 0)]
  transfers between devices with their start and end apart: 2 -> 3, of which waited for: 1 -> 2; matrix products, arithmetic and copies ran while one was open for 3% -> 4% of each run, Pallas kernels for 0% -> 0%
where the time goes in v1:
time: 528 us; the launch traced here: 527 us
  blocking collectives  315 us (60%)
  waiting for transfers between devices  90.7 us (17%)
  other arithmetic  35.9 us (7%)
  matrix products  30.4 us (6%)
  local copies, waits for them, and re-layouts  28 us (5%)
  between operations  14.9 us (3%)
  starting transfers between devices  11.9 us (2%)
    pmax x1, blocking collectives, local(): whole_top = lax.pmax(src_top, 'col')  112 us
    psum x1, blocking collectives, local(): src_total = lax.psum(src_total * jnp.exp(src_top - whole_top), 'col')  111 us
    all_gather x1, waiting for transfers between devices, local(): lax.all_gather(sources, 'col', axis=0, tiled=True)  86.5 us
    pmax x1, blocking collectives, local(): whole_tgt = lax.pmax(tgt_top, 'row')  68.4 us
    dot_general x1, matrix products, cost_blocks(): jnp.einsum('kid,kjd->kij', src_rows, tgt_rows, precision=lax.Precision.HI...  29.9 us
    psum x1, blocking collectives, local(): tgt_total = lax.psum(tgt_total * jnp.exp(tgt_top - whole_tgt), 'row')  12.7 us
    all_gather x1, blocking collectives, local(): lax.all_gather(g_pot, 'row', axis=0, tiled=True)  12 us
    all_to_all x1, starting transfers between devices, local(): lax.all_to_all(jnp.stack([log_a] * lax.axis_size('col')), 'col', 0, 0)  11.9 us
  transfers between devices with their start and end apart: 3, of which 2 were waited for; matrix products, arithmetic and copies ran while one was open for 4% of the time, Pallas kernels for 0%

profile of v1, /device:TPU:1, one launch (start us, length us, event | category | flops | bytes accessed | tf_op | source)
XLA Modules:
  0.0 527.1 jit_solution(12471940825700368541)
XLA Ops:
  7.2 0.0 all-gather.6.cloned.1.call-start
  7.2 0.7 all-gather.6.cloned.1.call-update
  7.9 0.0 all-gather.4.cloned.1.call-start
  7.9 0.7 all-gather.4.cloned.1.call-update
  8.6 1.3 stack.2
  9.9 11.9 %all-to-all-start = ((f32[32,1,256]{2,1,0:T(1,128)}), f32[32,1,256]{2,1,0:T(1,128)S(1)}, u32[]{:S(2)}, u32[]{:S(2)}) async-start(f32[32,1,256]{2,1,0:T(1,128)} %stack.2), calls=%async_computation | async-start | bytes 65536 | tf_op jit(solution)/shard_map/all_to_all | solution.py:41
  21.8 12.0 %all-gather = f32[8,1,256]{2,1,0:T(1,128)S(1)} all-gather(f32[1,1,256]{2,1,0:T(1,128)} %bitcast.31), channel_id=1, replica_groups=mesh['row'=8,'col'=32] {'row'}, dimensions={0}, use_global_device_ids=true | all-gather | bytes 9216 | tf_op jit(solution)/shard_map/all_gather | solution.py:36
  34.5 0.7 compare_select_fusion.1
  35.1 0.7 gather_fusion.2
  35.8 0.7 compare_and_fusion.1
  36.5 0.7 compare_select_fusion
  37.1 0.7 compare_and_fusion
  37.8 0.7 fusion.37
  38.5 0.7 fusion.36
  39.1 0.0 all-to-all-done
  39.2 2.7 all-gather.6.cloned.1.call-done
  41.9 1.9 multiply_reduce_fusion.1
  43.9 0.7 gather_fusion.4
  44.5 10.4 %gather_fusion.1 = f32[64,256,256]{2,1,0:T(8,128)} fusion(f32[8,256,256]{2,1,0:T(8,128)} %bitcast.19, s32[1024]{0:T(1024)S(1)} %pad_clamp_fusion.1), kind=kCustom, calls=%fused_computation.7 | custom fusion | bytes 33554688 | tf_op jit(solution)/shard_map/jit(_take)/gather | solution.py:52
  54.9 0.1 broadcast_select_fusion.3
  55.0 86.5 %all-gather.4.cloned.1.call-done = f32[8192,256]{1,0:T(8,128)} async-done(((f32[256,256]{1,0:T(8,128)}), f32[8192,256]{1,0:T(8,128)}) %all-gather.4.cloned.1.call-update) | async-done | bytes 8388624 | tf_op jit(solution)/shard_map/all_gather | solution.py:39
  141.6 4.5 multiply_reduce_fusion
  146.1 0.7 gather_fusion.3
  146.8 11.6 %gather_fusion = f32[64,256,256]{2,1,0:T(8,128)} fusion(f32[32,256,256]{2,1,0:T(8,128)} %bitcast.20, s32[1024]{0:T(1024)S(1)} %pad_clamp_fusion), kind=kCustom, calls=%fused_computation.6 | custom fusion | bytes 33554688 | tf_op jit(solution)/shard_map/jit(_take)/gather | solution.py:51
  158.4 0.1 broadcast_select_fusion.2
  158.5 29.9 %fusion.3 = (f32[64,256]{1,0:T(8,128)S(1)}, f32[64,256,256]{2,1,0:T(8,128)}) fusion(f32[64,256]{1,0:T(8,128)S(1)} %get-tuple-element.4, f32[64,256,256]{2,1,0:T(8,128)} %gather_fusion.1, pred[64]{0:T(512)(128)(4,1)S(1)} %compare_and_fusion.1, f32[64,256,256]{2,1,0:T(8,128)} %gather_fusion, pred[64]{0:T(512)(128)(4,1)S(1)} %compare_and_fusion, ...), kind=kOutput, calls=%fused_computation.16 | convolution fusion | flops 12922634240 | bytes 50593920 | tf_op jit(solution)/shard_map/kid,kjd->kij/dot_general | solution.py:16
  188.4 8.5 %exponential_reduce_fusion.1 = f32[64,256]{1,0:T(8,128)S(1)} fusion(f32[64,256,256]{2,1,0:T(8,128)} %get-tuple-element.7, f32[64,256]{1,0:T(8,128)S(1)} %get-tuple-element.6, f32[64,256]{1,0:T(8,128)S(1)} %get-tuple-element.4), kind=kLoop, calls=%fused_computation.10 | loop fusion | flops 16760832 | bytes 16973824 | tf_op jit(solution)/shard_map/reduce_sum | solution.py:59
  196.9 0.5 select_reduce_fusion
  197.4 0.7 gather_fusion.5
  198.1 0.0 copy-done.1
  198.1 0.3 convolution_bitcast_fusion
  198.4 111.5 %pmax.14 = f32[8192]{0:T(1024)S(1)} all-reduce(f32[8192]{0:T(1024)S(1)} %bitcast.24), channel_id=1, replica_groups=mesh['row'=8,'col'=32] {'col'}, use_global_device_ids=true, to_apply=%region_4.7 | all-reduce | flops 8192 | bytes 65536 | tf_op jit(solution)/shard_map/pmax | solution.py:61
  310.0 110.7 %psum.14 = f32[8192]{0:T(1024)S(1)} all-reduce(f32[8192]{0:T(1024)S(1)} %exponential_multiply_fusion), channel_id=1, replica_groups=mesh['row'=8,'col'=32] {'col'}, use_global_device_ids=true, to_apply=%region_6.9 | all-reduce | flops 8192 | bytes 65536 | tf_op jit(solution)/shard_map/psum | solution.py:62
  420.7 0.7 gather_fusion.6
  421.4 0.1 broadcast_select_fusion
  421.5 0.0 copy-start.2
  421.5 0.0 copy-start
  421.5 7.2 %fusion.4 = f32[64,256]{1,0:T(8,128)S(1)} fusion(f32[64,256,256]{2,1,0:T(8,128)} %get-tuple-element.7, f32[64,256]{1,0:T(8,128)S(1)} %broadcast_select_fusion), kind=kLoop, calls=%fused_computation.17 | loop fusion | flops 12566528 | bytes 16908288 | tf_op jit(solution)/shard_map/reduce_max | solution.py:68
  428.7 8.0 %exponential_reduce_fusion = f32[64,256]{1,0:T(8,128)S(1)} fusion(f32[64,256,256]{2,1,0:T(8,128)} %get-tuple-element.7, f32[64,256]{1,0:T(8,128)S(1)} %fusion.4, f32[64,256]{1,0:T(8,128)S(1)} %broadcast_select_fusion), kind=kLoop, calls=%fused_computation.8 | loop fusion | flops 16760832 | bytes 16973824 | tf_op jit(solution)/shard_map/reduce_sum | solution.py:69
  436.8 0.1 select_reduce_fusion.1
  436.9 0.7 gather_fusion.7
  437.6 0.0 copy-done.2
  437.6 0.3 convolution_bitcast_fusion.1
  437.9 68.4 %pmax.15 = f32[2048]{0:T(1024)S(1)} all-reduce(f32[2048]{0:T(1024)S(1)} %bitcast.28), channel_id=1, replica_groups=mesh['row'=8,'col'=32] {'row'}, use_global_device_ids=true, to_apply=%region_9.12 | all-reduce | flops 2048 | bytes 16384 | tf_op jit(solution)/shard_map/pmax | solution.py:71
  506.3 12.7 %psum.15 = f32[2048]{0:T(1024)S(1)} all-reduce(f32[2048]{0:T(1024)S(1)} %exponential_multiply_fusion.1), channel_id=1, replica_groups=mesh['row'=8,'col'=32] {'row'}, use_global_device_ids=true, to_apply=%region_11.14 | all-reduce | flops 2048 | bytes 16384 | tf_op jit(solution)/shard_map/psum | solution.py:72
  519.0 0.6 dynamic_slice.9
  519.6 0.0 copy-done
  519.6 0.6 multiply_subtract_fusion.1
  (16 shorter events, 0.2 us)
Async XLA Ops:
  7.2 34.8 %all-gather.6.cloned.1.call-start = ((), (), s32[]{:S(2)}) async-start(), calls=%async_computation.2 | async-start | bytes 2359296 | tf_op jit(solution)/shard_map/all_gather | solution.py:35
  7.9 133.7 %all-gather.4.cloned.1.call-start = ((), (), s32[]{:S(2)}) async-start(), calls=%async_computation.1 | async-start | bytes 8650752 | tf_op jit(solution)/shard_map/all_gather | solution.py:39
  9.9 29.2 %all-to-all-start = ((f32[32,1,256]{2,1,0:T(1,128)}), f32[32,1,256]{2,1,0:T(1,128)S(1)}, u32[]{:S(2)}, u32[]{:S(2)}) async-start(f32[32,1,256]{2,1,0:T(1,128)} %stack.2), calls=%async_computation | async-start | bytes 65536 | tf_op jit(solution)/shard_map/all_to_all | solution.py:41
  188.4 9.7 %copy-start.1 = (s32[64]{0:T(128)S(1)}, s32[64]{0:T(128)}, u32[]{:S(2)}) copy-start(s32[64]{0:T(128)} %param.17) | copy-start | bytes 772
  421.5 16.1 %copy-start.2 = (s32[64]{0:T(128)S(1)}, s32[64]{0:T(128)}, u32[]{:S(2)}) copy-start(s32[64]{0:T(128)} %param.18) | copy-start | bytes 772
  421.5 98.1 %copy-start = (f32[256]{0:T(256)S(1)}, f32[256]{0:T(256)}, u32[]{:S(2)}) copy-start(f32[256]{0:T(256)} %param.16) | copy-start | bytes 3076
Sparse Core Ops, SparseCore 0:
  9.8 32.0 all-gather.5
  44.5 96.9 all-gather.3
